TPU v7x, 256 devices: a whole 4x4x8 slice. The times are simulated.
256 devices in a mesh: row: 16 (over x, z_lo, core), col: 16 (over z_hi, y).
Axes of the slice: x: 4, y: 4, z: 8 (z_hi: 4, z_lo: 2; z = z_hi * 2 + z_lo), core: 2. Of those that a mesh axis runs over, the one named last changes fastest.
Arguments:
- amplitudes: bfloat16 [4, 1024, 1024], P(None, 'row', 'col'), may hold values from -6 to 6
- factors: bfloat16 [3072, 65536], P('col', 'row'), may hold values from -0.029907227 to 0.029907227
- tile_mask: int32 [16, 16], replicated, may hold values 0 or 1
- tile_irrep: int32 [16], replicated, may hold values from 0 to 1
Outputs:
- residual: float32 [4, 64, 64], P(None, 'row', 'col')
All inputs are finite; a program needn't handle non-finite values.
Results may differ from a plain program's by a relative error of at most 0.007.
Values may be sent and summed in bfloat16 or wider, within the bound.
A program may use at most 128 MiB of HBM per device.

v0:
```python
import jax
import jax.numpy as jnp
from jax import lax
from jax.sharding import PartitionSpec as P

TILE = 64
NOCC = 2
WIN = 64


def mirrored(values):
    pair_count, rows_here, cols_here = values.shape
    return (
        values.reshape(NOCC, NOCC, rows_here, cols_here)
        .transpose(1, 0, 3, 2)
        .reshape(pair_count, cols_here, rows_here)
    )


def reduce_all(values):
    by_cols = lax.psum_scatter(values, "col", scatter_dimension=2, tiled=True)
    return lax.psum_scatter(by_cols, "row", scatter_dimension=1, tiled=True)


def contract(running, near_side, masked, far_flat, q_step):
    q_count = near_side.shape[0]
    far_piece = far_flat.reshape(q_count, far_flat.shape[1] // WIN, WIN)

    def one_block(step_index, summed):
        near_block = lax.dynamic_slice_in_dim(near_side, step_index * q_step, q_step, 0)
        far_block = lax.dynamic_slice_in_dim(far_piece, step_index * q_step, q_step, 0)
        partial_value = jnp.einsum(
            "qkca,pkcd->qpkad", near_block, masked, preferred_element_type=jnp.float32
        ).astype(jnp.bfloat16)
        return summed + jnp.einsum(
            "qpkad,qdb->pab", partial_value, far_block, preferred_element_type=jnp.float32
        )

    return lax.fori_loop(0, q_count // q_step, one_block, running)


def per_device(amplitudes, factors, tile_mask, tile_irrep):
    pair_count = amplitudes.shape[0]
    q_cols = factors.shape[0]
    rows_virt = factors.shape[1] // WIN
    tile_count = tile_mask.shape[0]
    tiles_here = rows_virt // TILE
    pair_index = jnp.arange(pair_count, dtype=jnp.int32)
    pair_irrep = jnp.bitwise_xor(pair_index // NOCC % 2, pair_index % NOCC % 2)
    cross_irrep = jnp.bitwise_xor(tile_irrep[:, None], tile_irrep[None, :])
    live_tiles = tile_mask[None, :, :] * (
        cross_irrep[None, :, :] == pair_irrep[:, None, None]
    ).astype(jnp.int32)
    amp_row = lax.all_gather(amplitudes, "col", axis=2, tiled=True)
    start_sum = jnp.zeros((pair_count, WIN, WIN), jnp.float32)
    own_tiles = lax.dynamic_slice_in_dim(
        live_tiles, lax.axis_index("row") * tiles_here, tiles_here, 1
    )
    shaped = amp_row.reshape(pair_count, tiles_here, TILE, tile_count, TILE)
    masked = (shaped * own_tiles.astype(jnp.bfloat16)[:, :, None, :, None]).reshape(
        pair_count, tiles_here, TILE, tile_count * TILE
    )
    near_side = factors.reshape(q_cols, tiles_here, TILE, WIN)
    far_all = lax.all_gather(factors, "row", axis=1, tiled=True)
    ladder = contract(start_sum, near_side, masked, far_all, 16)
    own_block = reduce_all(ladder)
    b_count = own_block.shape[2]
    grid_row = lax.all_gather(own_block, "col", axis=2, tiled=True)
    swapped = lax.all_to_all(grid_row, "row", split_axis=2, concat_axis=1, tiled=True)
    wanted = lax.dynamic_slice_in_dim(swapped, lax.axis_index("col") * b_count, b_count, 1)
    return own_block + mirrored(wanted)


def solution(mesh):
    return jax.shard_map(
        per_device,
        mesh=mesh,
        in_specs=(P(None, "row", "col"), P("col", "row"), P(), P()),
        out_specs=P(None, "row", "col"),
        check_vma=False,
    )
```

profile of v0, /device:TPU:1, one launch (start us, length us, event | category | flops | bytes accessed | tf_op | source)
XLA Modules:
  0.0 609.0 jit_solution(5877241851750673732)
XLA Ops:
  6.5 0.0 all-gather.2.cloned.1.call-start
  6.5 0.7 all-gather.2.cloned.1.call-update
  7.3 0.0 all-reduce.4.cloned.1.call-start
  7.3 3.2 copy.21
  10.5 0.8 broadcast_xor_fusion
  11.3 0.7 constant_dynamic-slice_fusion.2
  12.0 0.1 fusion.25
  12.1 0.1 copy.23
  12.2 0.9 copy.22
  13.1 55.8 %all_gather.9 = bf16[4,64,1024]{1,0,2:T(4,128)(2,1)S(1)} all-gather(bf16[4,64,64]{1,0,2:T(4,128)(2,1)S(1)} %copy.22), channel_id=1, replica_groups=mesh['row'=16,'col'=16] {'col'}, dimensions={2}, use_global_device_ids=true | all-gather | bytes 557056 | tf_op jit(solution)/shard_map/all_gather | solution.py:54
  69.0 4.2 multiply_bitcast_fusion
  73.1 1.3 copy.26
  74.5 5.1 copy.25
  79.6 83.9 %all-gather.2.cloned.1.call-done = bf16[192,65536]{1,0:T(8,128)(2,1)} async-done(((bf16[192,4096]{1,0:T(8,128)(2,1)}), bf16[192,65536]{1,0:T(8,128)(2,1)}) %all-gather.2.cloned.1.call-update) | async-done | bytes 25165840 | tf_op jit(solution)/shard_map/all_gather | solution.py:64
  163.5 36.1 %copy.24 = bf16[192,65536]{0,1:T(8,128)(2,1)} copy(bf16[192,65536]{1,0:T(8,128)(2,1)} %all-gather.2.cloned.1.call-done) | data formatting | bytes 50331648 | tf_op jit(solution)/shard_map/all_gather | solution.py:64
  199.6 0.0 copy-start
  199.6 49.3 %copy.27 = bf16[192,1024,64]{1,2,0:T(8,128)(2,1)} copy(bf16[192,1024,64]{0,2,1:T(8,128)(2,1)} %bitcast.73) | data formatting | bytes 50331648
  248.8 0.0 copy-done
  248.8 0.0 copy-start.2
  248.8 0.0 copy-start.1
  248.8 75.0 %while.14 = (s32[]{:T(128)}, f32[4,64,64]{2,1,0:T(8,128)S(1)}, bf16[192,1,64,64]{2,3,0,1:T(8,128)(2,1)}, bf16[4,1,64,1024]{3,2,0,1:T(8,128)(2,1)S(1)}, bf16[192,...) while((s32[]{:T(128)}, f32[4,64,64]{2,1,0:T(8,128)S(1)}, ...), condition=%wide.region_1.2_spmd.clone, body=%wide.region_0.1_spmd.clone.sunk | while | flops 1077968896 | bytes 3016340 | solution.py:39
  248.9 6.2 %fusion.38 = f32[4,64,64]{2,1,0:T(8,128)S(1)} fusion(bf16[192,1024,64]{1,2,0:T(8,128)(2,1)} %get-tuple-element.198, s32[]{:T(128)S(6)} %select_n.74, bf16[4,1,64,1024]{3,2,0,1:T(8,128)(2,1)S(1)} %get-tuple-element.197, bf16[192,1,64,64]{2,3,0,1:T(8,128)(2,1)} %get-tuple-element.196, f32[4,64,64]{2,1,0:T(8,128)S(1)} %get-tuple-element.186, ...), kind=kOutput, calls=%fused_computation.7.clone.1 | convolution fusion | flops 1077968896 | bytes 3016192 | tf_op jit(solution)/shard_map/while/body/eval_jaxpr/qpkad,qdb->pab/dot_general | solution.py:35
  255.1 6.2 %fusion.38 = f32[4,64,64]{2,1,0:T(8,128)S(1)} fusion(bf16[192,1024,64]{1,2,0:T(8,128)(2,1)} %get-tuple-element.198, s32[]{:T(128)S(6)} %select_n.74, bf16[4,1,64,1024]{3,2,0,1:T(8,128)(2,1)S(1)} %get-tuple-element.197, bf16[192,1,64,64]{2,3,0,1:T(8,128)(2,1)} %get-tuple-element.196, f32[4,64,64]{2,1,0:T(8,128)S(1)} %get-tuple-element.186, ...), kind=kOutput, calls=%fused_computation.7.clone.1 | convolution fusion | flops 1077968896 | bytes 3016192 | tf_op jit(solution)/shard_map/while/body/eval_jaxpr/qpkad,qdb->pab/dot_general | solution.py:35
  261.4 6.2 %fusion.38 = f32[4,64,64]{2,1,0:T(8,128)S(1)} fusion(bf16[192,1024,64]{1,2,0:T(8,128)(2,1)} %get-tuple-element.198, s32[]{:T(128)S(6)} %select_n.74, bf16[4,1,64,1024]{3,2,0,1:T(8,128)(2,1)S(1)} %get-tuple-element.197, bf16[192,1,64,64]{2,3,0,1:T(8,128)(2,1)} %get-tuple-element.196, f32[4,64,64]{2,1,0:T(8,128)S(1)} %get-tuple-element.186, ...), kind=kOutput, calls=%fused_computation.7.clone.1 | convolution fusion | flops 1077968896 | bytes 3016192 | tf_op jit(solution)/shard_map/while/body/eval_jaxpr/qpkad,qdb->pab/dot_general | solution.py:35
  267.6 6.2 %fusion.38 = f32[4,64,64]{2,1,0:T(8,128)S(1)} fusion(bf16[192,1024,64]{1,2,0:T(8,128)(2,1)} %get-tuple-element.198, s32[]{:T(128)S(6)} %select_n.74, bf16[4,1,64,1024]{3,2,0,1:T(8,128)(2,1)S(1)} %get-tuple-element.197, bf16[192,1,64,64]{2,3,0,1:T(8,128)(2,1)} %get-tuple-element.196, f32[4,64,64]{2,1,0:T(8,128)S(1)} %get-tuple-element.186, ...), kind=kOutput, calls=%fused_computation.7.clone.1 | convolution fusion | flops 1077968896 | bytes 3016192 | tf_op jit(solution)/shard_map/while/body/eval_jaxpr/qpkad,qdb->pab/dot_general | solution.py:35
  273.9 6.2 %fusion.38 = f32[4,64,64]{2,1,0:T(8,128)S(1)} fusion(bf16[192,1024,64]{1,2,0:T(8,128)(2,1)} %get-tuple-element.198, s32[]{:T(128)S(6)} %select_n.74, bf16[4,1,64,1024]{3,2,0,1:T(8,128)(2,1)S(1)} %get-tuple-element.197, bf16[192,1,64,64]{2,3,0,1:T(8,128)(2,1)} %get-tuple-element.196, f32[4,64,64]{2,1,0:T(8,128)S(1)} %get-tuple-element.186, ...), kind=kOutput, calls=%fused_computation.7.clone.1 | convolution fusion | flops 1077968896 | bytes 3016192 | tf_op jit(solution)/shard_map/while/body/eval_jaxpr/qpkad,qdb->pab/dot_general | solution.py:35
  280.1 6.2 %fusion.38 = f32[4,64,64]{2,1,0:T(8,128)S(1)} fusion(bf16[192,1024,64]{1,2,0:T(8,128)(2,1)} %get-tuple-element.198, s32[]{:T(128)S(6)} %select_n.74, bf16[4,1,64,1024]{3,2,0,1:T(8,128)(2,1)S(1)} %get-tuple-element.197, bf16[192,1,64,64]{2,3,0,1:T(8,128)(2,1)} %get-tuple-element.196, f32[4,64,64]{2,1,0:T(8,128)S(1)} %get-tuple-element.186, ...), kind=kOutput, calls=%fused_computation.7.clone.1 | convolution fusion | flops 1077968896 | bytes 3016192 | tf_op jit(solution)/shard_map/while/body/eval_jaxpr/qpkad,qdb->pab/dot_general | solution.py:35
  286.4 6.2 %fusion.38 = f32[4,64,64]{2,1,0:T(8,128)S(1)} fusion(bf16[192,1024,64]{1,2,0:T(8,128)(2,1)} %get-tuple-element.198, s32[]{:T(128)S(6)} %select_n.74, bf16[4,1,64,1024]{3,2,0,1:T(8,128)(2,1)S(1)} %get-tuple-element.197, bf16[192,1,64,64]{2,3,0,1:T(8,128)(2,1)} %get-tuple-element.196, f32[4,64,64]{2,1,0:T(8,128)S(1)} %get-tuple-element.186, ...), kind=kOutput, calls=%fused_computation.7.clone.1 | convolution fusion | flops 1077968896 | bytes 3016192 | tf_op jit(solution)/shard_map/while/body/eval_jaxpr/qpkad,qdb->pab/dot_general | solution.py:35
  292.6 6.2 %fusion.38 = f32[4,64,64]{2,1,0:T(8,128)S(1)} fusion(bf16[192,1024,64]{1,2,0:T(8,128)(2,1)} %get-tuple-element.198, s32[]{:T(128)S(6)} %select_n.74, bf16[4,1,64,1024]{3,2,0,1:T(8,128)(2,1)S(1)} %get-tuple-element.197, bf16[192,1,64,64]{2,3,0,1:T(8,128)(2,1)} %get-tuple-element.196, f32[4,64,64]{2,1,0:T(8,128)S(1)} %get-tuple-element.186, ...), kind=kOutput, calls=%fused_computation.7.clone.1 | convolution fusion | flops 1077968896 | bytes 3016192 | tf_op jit(solution)/shard_map/while/body/eval_jaxpr/qpkad,qdb->pab/dot_general | solution.py:35
  298.9 6.2 %fusion.38 = f32[4,64,64]{2,1,0:T(8,128)S(1)} fusion(bf16[192,1024,64]{1,2,0:T(8,128)(2,1)} %get-tuple-element.198, s32[]{:T(128)S(6)} %select_n.74, bf16[4,1,64,1024]{3,2,0,1:T(8,128)(2,1)S(1)} %get-tuple-element.197, bf16[192,1,64,64]{2,3,0,1:T(8,128)(2,1)} %get-tuple-element.196, f32[4,64,64]{2,1,0:T(8,128)S(1)} %get-tuple-element.186, ...), kind=kOutput, calls=%fused_computation.7.clone.1 | convolution fusion | flops 1077968896 | bytes 3016192 | tf_op jit(solution)/shard_map/while/body/eval_jaxpr/qpkad,qdb->pab/dot_general | solution.py:35
  305.2 6.2 %fusion.38 = f32[4,64,64]{2,1,0:T(8,128)S(1)} fusion(bf16[192,1024,64]{1,2,0:T(8,128)(2,1)} %get-tuple-element.198, s32[]{:T(128)S(6)} %select_n.74, bf16[4,1,64,1024]{3,2,0,1:T(8,128)(2,1)S(1)} %get-tuple-element.197, bf16[192,1,64,64]{2,3,0,1:T(8,128)(2,1)} %get-tuple-element.196, f32[4,64,64]{2,1,0:T(8,128)S(1)} %get-tuple-element.186, ...), kind=kOutput, calls=%fused_computation.7.clone.1 | convolution fusion | flops 1077968896 | bytes 3016192 | tf_op jit(solution)/shard_map/while/body/eval_jaxpr/qpkad,qdb->pab/dot_general | solution.py:35
  311.4 6.2 %fusion.38 = f32[4,64,64]{2,1,0:T(8,128)S(1)} fusion(bf16[192,1024,64]{1,2,0:T(8,128)(2,1)} %get-tuple-element.198, s32[]{:T(128)S(6)} %select_n.74, bf16[4,1,64,1024]{3,2,0,1:T(8,128)(2,1)S(1)} %get-tuple-element.197, bf16[192,1,64,64]{2,3,0,1:T(8,128)(2,1)} %get-tuple-element.196, f32[4,64,64]{2,1,0:T(8,128)S(1)} %get-tuple-element.186, ...), kind=kOutput, calls=%fused_computation.7.clone.1 | convolution fusion | flops 1077968896 | bytes 3016192 | tf_op jit(solution)/shard_map/while/body/eval_jaxpr/qpkad,qdb->pab/dot_general | solution.py:35
  317.7 6.2 %fusion.38 = f32[4,64,64]{2,1,0:T(8,128)S(1)} fusion(bf16[192,1024,64]{1,2,0:T(8,128)(2,1)} %get-tuple-element.198, s32[]{:T(128)S(6)} %select_n.74, bf16[4,1,64,1024]{3,2,0,1:T(8,128)(2,1)S(1)} %get-tuple-element.197, bf16[192,1,64,64]{2,3,0,1:T(8,128)(2,1)} %get-tuple-element.196, f32[4,64,64]{2,1,0:T(8,128)S(1)} %get-tuple-element.186, ...), kind=kOutput, calls=%fused_computation.7.clone.1 | convolution fusion | flops 1077968896 | bytes 3016192 | tf_op jit(solution)/shard_map/while/body/eval_jaxpr/qpkad,qdb->pab/dot_general | solution.py:35
  323.9 0.8 copy.28
  324.7 0.0 all-reduce.4.cloned.1.call-update
  324.7 0.0 copy-done.2
  324.7 0.6 dynamic-slice
  325.3 0.0 copy-done.1
  325.3 0.6 dynamic-slice.2
  327.2 152.6 %all-reduce.4.cloned.1.call-done = f32[4,64,64]{1,0,2:T(4,128)} async-done(((f32[4,64,64]{1,0,2:T(4,128)}), f32[4,64,64]{1,0,2:T(4,128)}) %all-reduce.4.cloned.1.call-update) | async-done | bytes 65552
  479.8 0.7 constant_dynamic-slice_fusion.1
  480.5 0.1 copy.29
  480.6 60.3 %all-reduce.1 = f32[4,64,4]{2,1,0:T(8,128)S(1)} all-reduce(f32[4,64,4]{2,1,0:T(8,128)S(1)} %copy.29), channel_id=3, replica_groups=mesh['row'=16,'col'=16] {'row'}, use_global_device_ids=true, to_apply=%region_3.4.clone | all-reduce | flops 1024 | bytes 8192
  540.9 0.1 copy.30
  541.0 39.3 %all_gather.11 = f32[4,4,64]{1,0,2:T(4,128)} all-gather(f32[4,4,4]{1,0,2:T(4,128)S(1)} %copy.30), channel_id=1, replica_groups=mesh['row'=16,'col'=16] {'col'}, dimensions={2}, use_global_device_ids=true | all-gather | bytes 4352 | tf_op jit(solution)/shard_map/all_gather | solution.py:68
  580.4 14.7 %all-to-all-start = ((f32[4,4,64]{1,0,2:T(4,128)}), f32[4,4,64]{1,0,2:T(4,128)S(1)}, u32[]{:S(2)}, u32[]{:S(2)}) async-start(f32[4,4,64]{1,0,2:T(4,128)} %all_gather.11), calls=%async_computation | async-start | bytes 262144 | tf_op jit(solution)/shard_map/all_to_all | solution.py:69
  595.0 6.2 %all-to-all-done = f32[4,4,64]{1,0,2:T(4,128)S(1)} async-done(((f32[4,4,64]{1,0,2:T(4,128)}), f32[4,4,64]{1,0,2:T(4,128)S(1)}, u32[]{:S(2)}, u32[]{:S(2)}) %all-to-all-start) | async-done | bytes 4128 | tf_op jit(solution)/shard_map/all_to_all | solution.py:69
  601.3 0.1 all_to_all.16
  601.4 0.1 constant_dynamic-slice_fusion.3
  601.5 0.6 bitcast_add_fusion
  (6 shorter events, 0.1 us)
Async XLA Ops:
  6.5 156.9 %all-gather.2.cloned.1.call-start = ((), (), s32[]{:S(2)}) async-start(), calls=%async_computation.1 | async-start | bytes 26738688 | tf_op jit(solution)/shard_map/all_gather | solution.py:64
  7.3 472.5 %all-reduce.4.cloned.1.call-start = ((), (), s32[]{:S(2)}) async-start(), calls=%async_computation.2 | async-start | bytes 262144
  199.6 49.3 %copy-start = (bf16[4,1,64,1024]{3,2,0,1:T(8,128)(2,1)S(1)}, bf16[4,1,64,1024]{3,2,0,1:T(8,128)(2,1)}, u32[]{:S(2)}) copy-start(bf16[4,1,64,1024]{3,2,0,1:T(8,128)(2,1)} %copy.26) | copy-start | bytes 1572868
  248.8 75.9 %copy-start.2 = (u32[256]{0:T(256)S(1)}, u32[256]{0:T(256)}, u32[]{:S(2)}) copy-start(u32[256]{0:T(256)} %constant.89) | copy-start | bytes 3076
  248.8 76.4 %copy-start.1 = (u32[256]{0:T(256)S(1)}, u32[256]{0:T(256)}, u32[]{:S(2)}) copy-start(u32[256]{0:T(256)} %constant.93) | copy-start | bytes 3076
  580.4 20.9 %all-to-all-start = ((f32[4,4,64]{1,0,2:T(4,128)}), f32[4,4,64]{1,0,2:T(4,128)S(1)}, u32[]{:S(2)}, u32[]{:S(2)}) async-start(f32[4,4,64]{1,0,2:T(4,128)} %all_gather.11), calls=%async_computation | async-start | bytes 262144 | tf_op jit(solution)/shard_map/all_to_all | solution.py:69
Sparse Core Ops, SparseCore 0:
  9.2 154.2 all-gather.1
  324.8 154.9 all-reduce.3
where the time goes:
time: 612 us; the launch traced here: 609 us
  waiting for transfers between devices  243 us (40%)
  blocking collectives  155 us (25%)
  local copies, waits for them, and re-layouts  99.9 us (16%)
  matrix products  74.7 us (12%)
  between operations  14.8 us (2%)
  starting transfers between devices  14.7 us (2%)
    unnamed x3, waiting for transfers between devices  153 us
    all_gather x1, waiting for transfers between devices, per_device(): far_all = lax.all_gather(factors, 'row', axis=1, tiled=True)  83.9 us
    dot_general x12, matrix products, one_block(): jnp.einsum('qpkad,qdb->pab', partial_value, far_block, preferred_element_...  74.7 us
    unnamed x15, local copies, waits for them, and re-layouts  61.8 us
    unnamed x1, blocking collectives  60.3 us
    all_gather x1, blocking collectives, per_device(): amp_row = lax.all_gather(amplitudes, 'col', axis=2, tiled=True)  55.8 us
    all_gather x1, blocking collectives, per_device(): grid_row = lax.all_gather(own_block, 'col', axis=2, tiled=True)  39.3 us
    all_gather x1, local copies, waits for them, and re-layouts, per_device(): far_all = lax.all_gather(factors, 'row', axis=1, tiled=True)  36.1 us
  transfers between devices with their start and end apart: 3, of which 3 were waited for; matrix products, arithmetic and copies ran while one was open for 3% of the time, Pallas kernels for 0%

commit v1 on v0

v1 whole, which is shorter than its diff:
```python
import functools

import jax
import jax.numpy as jnp
from jax import lax
from jax.experimental import pallas as pl
from jax.experimental.pallas import tpu as pltpu
from jax.sharding import PartitionSpec as P

TILE = 64
WIN = 64
MESH = pl.DeviceIdType.MESH
F32 = jnp.float32
BF16 = jnp.bfloat16


def greet(peers):
    barrier = pltpu.get_barrier_semaphore()
    for peer in peers:
        pl.semaphore_signal(barrier, inc=1, device_id=peer, device_id_type=MESH)
    pl.semaphore_wait(barrier, len(peers))


def row_swap(size, wide):
    at = lax.broadcasted_iota(jnp.int32, (size * size, size * size), 0)
    come = lax.broadcasted_iota(jnp.int32, (size * size, size * size), 1)
    hit = (at // size == come % size) & (at % size == come // size)
    return jnp.where(hit, 1.0, 0.0).astype(wide)


def regroup(fin, sbuf, g, swap):
    lane = lax.broadcasted_iota(jnp.int32, (16, 128), 1)
    low = lane < 64
    for jb in range(2):
        stacks = ([], [])
        for jj in range(16):
            cols = pl.ds(128 * (16 * jb + jj), 128)
            halves = ([], [])
            for kp in range(2):
                v0 = fin[pl.ds(64 * g + 32 * kp, 16), cols].astype(F32)
                v1 = fin[pl.ds(64 * g + 32 * kp + 16, 16), cols].astype(F32)
                halves[0].append(jnp.where(low, v0, pltpu.roll(v1, 64, 1)).astype(BF16))
                halves[1].append(jnp.where(low, pltpu.roll(v0, 64, 1), v1).astype(BF16))
            for e in range(2):
                stacks[e].append(jnp.concatenate(halves[e], axis=1))
        for e in range(2):
            moved = jnp.dot(swap, jnp.concatenate(stacks[e], axis=0), preferred_element_type=F32).astype(BF16)
            for r in range(16):
                sbuf[g, r, pl.ds(32 * e + 16 * jb, 16), :] = moved[16 * r : 16 * r + 16, :]


def share_kernel(f_hbm, fm, fin, sbuf, in_sem, send_sem, recv_sem, own_sem):
    row = lax.axis_index("row")
    col = lax.axis_index("col")
    loads = []
    for g in range(3):
        load = pltpu.make_async_copy(f_hbm.at[pl.ds(64 * g, 64)], fin.at[pl.ds(64 * g, 64)], in_sem.at[g])
        load.start()
        loads.append(load)
    greet([((row + o) % 16, col) for o in range(1, 16)])
    swap = row_swap(16, BF16)
    copies = []
    for g in range(3):
        loads[g].wait()
        regroup(fin, sbuf, g, swap)
        for o in range(1, 16):
            dest = (row + o) % 16
            copy = pltpu.make_async_remote_copy(
                src_ref=sbuf.at[g, dest],
                dst_ref=fm.at[g, row],
                send_sem=send_sem.at[g, o],
                recv_sem=recv_sem.at[g, o],
                device_id=(dest, col),
                device_id_type=MESH,
            )
            copy.start()
            copies.append(copy)
        own = pltpu.make_async_copy(sbuf.at[g, row], fm.at[g, row], own_sem.at[g])
        own.start()
        copies.append(own)
    for copy in copies:
        copy.wait()


def share(factors):
    return pl.pallas_call(
        share_kernel,
        out_shape=jax.ShapeDtypeStruct((3, 16, 64, 256), BF16),
        in_specs=[pl.BlockSpec(memory_space=pl.ANY)],
        out_specs=pl.BlockSpec(memory_space=pltpu.VMEM),
        scratch_shapes=[
            pltpu.VMEM((192, 4096), BF16),
            pltpu.VMEM((3, 16, 64, 256), BF16),
            pltpu.SemaphoreType.DMA((3,)),
            pltpu.SemaphoreType.DMA((3, 16)),
            pltpu.SemaphoreType.DMA((3, 16)),
            pltpu.SemaphoreType.DMA((3,)),
        ],
        compiler_params=pltpu.CompilerParams(collective_id=0, has_side_effects=True, vmem_limit_bytes=40 << 20),
        name="share_factors",
    )(factors)


def ladder_kernel(irrep, nt, lane_irrep, diag, fm, out, u0, u3, u1, xt, acc):
    lane = lax.broadcasted_iota(jnp.int32, (1, 1024), 1)
    lane2 = lax.broadcasted_iota(jnp.int32, (64, 128), 1)
    row2 = lax.broadcasted_iota(jnp.int32, (64, 128), 0)
    for t in range(16):
        rows = pl.ds(64 * t, 64)
        differs = jnp.abs(lane_irrep[...] - irrep[t].astype(F32))
        same = 1.0 - differs
        tile = nt[rows, :]
        u1[rows, :] = tile * differs.astype(BF16)
        u0[rows, :] = tile * jnp.where(lane < 64 * t, same, 0.0).astype(BF16)
        u3[rows, :] = tile * jnp.where(lane >= 64 * (t + 1), same, 0.0).astype(BF16)
        pair = pl.ds(128 * (t // 2), 128)
        here = nt[rows, pair]
        same_here = jnp.broadcast_to(1.0 - jnp.abs(lane_irrep[:, pair] - irrep[t].astype(F32)), (64, 128))
        offset = lane2 - 64 * (t % 2)
        in_tile = (offset >= 0) & (offset < 64)
        keep0 = (offset < 0) | (in_tile & (offset <= row2))
        keep3 = (offset >= 64) | (in_tile & (offset > row2))
        u0[rows, pair] = here * jnp.where(keep0, same_here, 0.0).astype(BF16)
        extra = jnp.where(offset == row2, jnp.broadcast_to(diag[:, pair], (64, 128)), 0.0)
        u3[rows, pair] = here * jnp.where(keep3, same_here, 0.0).astype(BF16) + extra.astype(BF16)
    acc[...] = jnp.zeros_like(acc)

    @pl.loop(0, 3)
    def _(g):
        near = fm.at[g]
        for i in range(4):
            rows = pl.ds(256 * i, 256)
            done = 256 * (i + 1)
            x0 = jnp.dot(u0[rows, :done], near[:done, :], preferred_element_type=F32)
            xt[rows, 0:256] = x0.astype(BF16)
            x3 = jnp.dot(u3[rows, 256 * i :], near[256 * i :, :], preferred_element_type=F32)
            xt[rows, 256:512] = x3.astype(BF16)
            x1 = jnp.dot(u1[rows, :], near[...], preferred_element_type=F32)
            xt[rows, 512:768] = x1.astype(BF16)
        acc[...] += lax.dot_general(near[...], xt[...], (((0,), (0,)), ((), ())), preferred_element_type=F32)

    for p in range(3):
        total = jnp.zeros((64, 64), F32)
        for k in range(4):
            total = total + acc[64 * k : 64 * k + 64, 256 * p + 64 * k : 256 * p + 64 * k + 64]
        out[p] = total


def ladder(irrep, nt, lane_irrep, diag, fm):
    vmem = pl.BlockSpec(memory_space=pltpu.VMEM)
    return pl.pallas_call(
        ladder_kernel,
        out_shape=jax.ShapeDtypeStruct((3, 64, 64), F32),
        in_specs=[pl.BlockSpec(memory_space=pltpu.SMEM), vmem, vmem, vmem, vmem],
        out_specs=vmem,
        scratch_shapes=[
            pltpu.VMEM((1024, 1024), BF16),
            pltpu.VMEM((1024, 1024), BF16),
            pltpu.VMEM((1024, 1024), BF16),
            pltpu.VMEM((1024, 768), BF16),
            pltpu.VMEM((256, 768), F32),
        ],
        compiler_params=pltpu.CompilerParams(vmem_limit_bytes=40 << 20),
        name="ladder_sums",
    )(irrep, nt, lane_irrep, diag, fm)


def reduce_kernel(g, out, send_a, recv_a, send_b, recv_b, sa, ra, sb, rb):
    row = lax.axis_index("row")
    col = lax.axis_index("col")
    greet([((row + o) % 16, col) for o in range(1, 16)] + [(row, (col + o) % 16) for o in range(1, 16)])
    near = (g[0] + g[0].T, g[2].T, g[2], g[1] + g[1].T)
    for r in range(16):
        for p in range(4):
            send_a[r, 4 * p : 4 * p + 4, :] = near[p][4 * r : 4 * r + 4, :]
    copies = []
    for o in range(1, 16):
        dest = (row + o) % 16
        copy = pltpu.make_async_remote_copy(
            src_ref=send_a.at[dest], dst_ref=recv_a.at[o], send_sem=sa.at[o], recv_sem=ra.at[o],
            device_id=(dest, col), device_id_type=MESH,
        )
        copy.start()
        copies.append(copy)
    total = send_a[row]
    for o in range(1, 16):
        copies[o - 1].wait_recv()
        total = total + recv_a[o]
    turned = total.T
    for c in range(16):
        send_b[c] = turned[4 * c : 4 * c + 4, :]
    for o in range(1, 16):
        dest = (col + o) % 16
        copy = pltpu.make_async_remote_copy(
            src_ref=send_b.at[dest], dst_ref=recv_b.at[o], send_sem=sb.at[o], recv_sem=rb.at[o],
            device_id=(row, dest), device_id_type=MESH,
        )
        copy.start()
        copies.append(copy)
    final = send_b[col]
    for o in range(1, 16):
        copies[14 + o].wait_recv()
        final = final + recv_b[o]
    back = final.T
    for p in range(4):
        out[p] = back[4 * p : 4 * p + 4, :]
    for copy in copies:
        copy.wait_send()


def reduce(partial):
    vmem = pl.BlockSpec(memory_space=pltpu.VMEM)
    sems = pltpu.SemaphoreType.DMA((16,))
    return pl.pallas_call(
        reduce_kernel,
        out_shape=jax.ShapeDtypeStruct((4, 4, 4), F32),
        in_specs=[vmem],
        out_specs=vmem,
        scratch_shapes=[
            pltpu.VMEM((16, 16, 64), F32),
            pltpu.VMEM((16, 16, 64), F32),
            pltpu.VMEM((16, 4, 16), F32),
            pltpu.VMEM((16, 4, 16), F32),
            sems, sems, sems, sems,
        ],
        compiler_params=pltpu.CompilerParams(collective_id=1, has_side_effects=True),
        name="reduce_ladder",
    )(partial)


def regrouped(matrix):
    return matrix.reshape(32, 2, 32, 2).transpose(1, 0, 3, 2).reshape(64, 64)


def per_device(amplitudes, factors, tile_mask, tile_irrep):
    row = lax.axis_index("row")
    col = lax.axis_index("col")
    crossed = jnp.bitwise_xor(tile_irrep[row], tile_irrep[col])
    stored = tile_mask[row, col].astype(F32)
    amps = amplitudes.astype(F32) * stored
    alike = crossed == 0
    kept = jnp.where(alike, jnp.where(row <= col, amps[0], amps[3]), amps[1])
    given = jnp.where(alike, jnp.where(row <= col, amps[3], amps[0]), amps[2])
    pairs = [(r * 16 + c, c * 16 + r) for r in range(16) for c in range(16)]
    got = lax.ppermute(given.astype(BF16), ("row", "col"), pairs).astype(F32)
    at = lax.broadcasted_iota(jnp.int32, (64, 64), 0)
    to = lax.broadcasted_iota(jnp.int32, (64, 64), 1)
    a0 = regrouped(amps[0])
    a3 = regrouped(amps[3])
    diagonal = jnp.where(at < to, a0 + a0.T, jnp.where(at > to, a3 + a3.T, a0))
    piece = jnp.where(row == col, diagonal, regrouped(kept) + regrouped(got).T)
    column = lax.all_gather(piece.T.astype(BF16), "row", axis=1, tiled=True)
    nt = lax.all_gather(column, "col", axis=0, tiled=True)
    own_diag = jnp.where(row == col, jnp.diagonal(a3), 0.0)
    diag = lax.psum(own_diag, "row")
    diag = lax.all_gather(diag, "col", axis=0, tiled=True).reshape(1, 1024)
    lane_irrep = jnp.repeat(tile_irrep.astype(F32), 64).reshape(1, 1024)
    fm = share(factors)
    partial = ladder(tile_irrep, nt, lane_irrep, diag, fm.reshape(3, 1024, 256))
    return reduce(partial)


def solution(mesh):
    return jax.shard_map(
        per_device,
        mesh=mesh,
        in_specs=(P(None, "row", "col"), P("col", "row"), P(), P()),
        out_specs=P(None, "row", "col"),
        check_vma=False,
    )
```

time: 612 us -> 188 us (0.31)
  waiting for transfers between devices: 243 us -> 0.03 us
  local copies, waits for them, and re-layouts: 99.9 us -> 17 us
  matrix products: 74.7 us -> 0 us
  blocking collectives: 155 us -> 88.9 us
  Pallas kernels: 0 us -> 57.7 us
  starting transfers between devices: 14.7 us -> 4.6 us
    unnamed x3 -> x1, waiting for transfers between devices: 153 us -> 0.02 us
    all_gather x1, waiting for transfers between devices: 83.9 us -> 0.01 us  [per_device(): nt = lax.all_gather(column, 'col', axis=0, tiled=True)]
    dot_general x12 -> x0, matrix products: 74.7 us -> none  [one_block(): jnp.einsum('qpkad,qdb->pab', partial_value, far_block, preferred_element_...]
    all_gather x2 -> x1, blocking collectives: 95.2 us -> 28.1 us  [per_device(): column = lax.all_gather(piece.T.astype(BF16), 'row', axis=1, tiled=True)]
    pallas_call x0 -> x3, Pallas kernels: none -> 57.7 us  [the longest x1 25.4 us: share(): pl.pallas_call(share_kernel, out_shape=jax.ShapeDtypeStruct((3, 16, 64, 2...]
    unnamed x15 -> x14, local copies, waits for them, and re-layouts: 61.8 us -> 4.34 us
    all_gather x1, local copies, waits for them, and re-layouts: 36.1 us -> 0.78 us  [per_device(): column = lax.all_gather(piece.T.astype(BF16), 'row', axis=1, tiled=True)]
    psum x0 -> x1, blocking collectives: none -> 28.7 us  [per_device(): diag = lax.psum(own_diag, 'row')]
  transfers between devices with their start and end apart: 3 -> 2, of which waited for: 3 -> 0; matrix products, arithmetic and copies ran while one was open for 3% -> 5% of each run, Pallas kernels for 0% -> 14%
where the time goes in v1:
time: 188 us; the launch traced here: 187 us
  blocking collectives  88.9 us (47%)
  Pallas kernels  57.7 us (31%)
  local copies, waits for them, and re-layouts  17 us (9%)
  between operations  16.2 us (9%)
  starting transfers between devices  4.6 us (2%)
  other arithmetic  2.47 us (1%)
    unnamed x1, blocking collectives  32.1 us
    psum x1, blocking collectives, per_device(): diag = lax.psum(own_diag, 'row')  28.7 us
    all_gather x1, blocking collectives, per_device(): column = lax.all_gather(piece.T.astype(BF16), 'row', axis=1, tiled=True)  28.1 us
    pallas_call x1, Pallas kernels, share(): pl.pallas_call(share_kernel, out_shape=jax.ShapeDtypeStruct((3, 16, 64, 2...  25.4 us
    pallas_call x1, Pallas kernels, reduce(): pl.pallas_call(reduce_kernel, out_shape=jax.ShapeDtypeStruct((4, 4, 4), F...  25.3 us
    pallas_call x1, Pallas kernels, ladder(): pl.pallas_call(ladder_kernel, out_shape=jax.ShapeDtypeStruct((3, 64, 64),...  7 us
    ppermute x1, starting transfers between devices, per_device(): got = lax.ppermute(given.astype(BF16), ('row', 'col'), pairs).astype(F32)  4.59 us
    unnamed x14, local copies, waits for them, and re-layouts  4.34 us
  transfers between devices with their start and end apart: 2, of which 0 were waited for; matrix products, arithmetic and copies ran while one was open for 5% of the time, Pallas kernels for 14%

profile of v1, /device:TPU:1, one launch (start us, length us, event | category | flops | bytes accessed | tf_op | source)
XLA Modules:
  0.0 187.0 jit_solution(5874887278802828209)
XLA Ops:
  6.5 0.0 all-gather.2.cloned.1.call-start
  6.5 1.3 dynamic_slice.9
  8.5 1.4 fusion.8
  11.2 0.9 convert_multiply_fusion
  12.1 4.6 %collective-permute-start = (bf16[64,64]{1,0:T(8,128)(2,1)S(1)}, bf16[64,64]{1,0:T(8,128)(2,1)S(1)}, u32[]{:S(2)}, u32[]{:S(2)}) collective-permute-start(bf16[64,64]{1,0:T(8,128)(2,1)S(1)} %fusion.6), channel_id=1, source_target_pairs={{0,0},{1,16},{2,32},{3,48},{4,64},{5,80},{6,96},{7,112},{8,128},{9... | collective-permute-start | bytes 24584 | tf_op jit(solution)/shard_map/ppermute | solution.py:245
  16.7 1.1 reshape_squeeze.7
  17.8 1.1 reshape_squeeze.6
  18.9 2.1 %squeeze.2 = f32[32,2,32,2]{3,2,1,0:T(8,128)} reshape(f32[1,64,64]{2,1,0:T(8,128)S(1)} %get-tuple-element.6) | data formatting | bytes 32768 | tf_op jit(solution)/shard_map/squeeze | solution.py:242
  20.9 1.6 select_bitcast_fusion
  22.5 0.5 copy.21
  23.0 0.1 reshape.37
  23.1 0.1 copy.22
  23.2 0.7 copy.19
  23.9 0.1 reshape.36
  24.0 0.1 copy.20
  24.1 0.5 copy.24
  24.5 0.1 reshape.38
  24.7 0.0 copy-start.3
  24.7 0.0 collective-permute-done
  24.7 1.1 reshape.44
  25.7 0.0 copy-start.1
  25.7 0.7 copy.25
  26.5 0.1 reshape.43
  26.6 28.1 %all_gather.9 = bf16[64,1024]{0,1:T(8,128)(2,1)S(1)} all-gather(bf16[64,64]{0,1:T(8,128)(2,1)S(1)} %fusion.5), channel_id=1, replica_groups=mesh['row'=16,'col'=16] {'row'}, dimensions={1}, use_global_device_ids=true | all-gather | bytes 139264 | tf_op jit(solution)/shard_map/all_gather | solution.py:252
  54.7 0.8 copy.26
  55.5 0.0 all-gather.2.cloned.1.call-update
  55.5 0.0 copy-done.3
  55.6 0.1 broadcast_in_dim.11
  55.6 0.1 reshape_reshape.3.lane_irrep
  55.7 0.8 gather_fusion
  56.5 0.0 copy-done.1
  56.5 0.0 copy-start.4
  56.6 25.4 %share_factors.1 = bf16[3,16,64,256]{3,2,1,0:T(8,128)(2,1)S(1)} custom-call(bf16[192,4096]{1,0:T(8,128)(2,1)S(1)} %copy-done.1), custom_call_target="tpu_custom_call" | custom-call | tf_op jit(solution)/shard_map/share_factors/pallas_call | solution.py:86
  82.0 0.0 copy-done.4
  82.0 0.6 dynamic-slice
  83.3 28.7 %psum.7 = f32[64]{0:T(128)S(1)} all-reduce(f32[64]{0:T(128)S(1)} %broadcast_select_fusion), channel_id=1, replica_groups=mesh['row'=16,'col'=16] {'row'}, use_global_device_ids=true, to_apply=%region_0.1 | all-reduce | flops 64 | bytes 512 | tf_op jit(solution)/shard_map/psum | solution.py:255
  112.0 0.2 dynamic-update-slice
  112.2 32.1 %all-reduce = f32[1024]{0:T(1024)S(1)} all-reduce(f32[1024]{0:T(1024)S(1)} %dynamic-update-slice), channel_id=1, replica_groups=mesh['row'=16,'col'=16] {'col'}, use_global_device_ids=true, to_apply=%add | all-reduce | flops 1024 | bytes 8192
  144.3 0.0 all-gather.2.cloned.1.call-done.nt
  144.3 0.0 copy-start
  144.3 1.6 copy-done
  145.9 7.0 %ladder_sums.1.g = f32[3,64,64]{2,1,0:T(8,128)S(1)} custom-call(s32[16]{0:T(128)S(1)} %copy-done.3, bf16[1024,1024]{1,0:T(8,128)(2,1)S(1)} %copy-done, f32[1,1024]{1,0:T(1,128)S(1)} %reshape_reshape.3.lane_irrep, f32[1,1024]{1,0:T(1,128)S(1)} %bitcast.45, bf16[3,1024,256]{2,1,0:T(8,128)(2,1)S(1)} %bitcast.44), custom_call_target="tpu_custom_call" | custom-call | tf_op jit(solution)/shard_map/ladder_sums/pallas_call | solution.py:151
  152.9 0.0 copy-start.2
  153.0 0.6 copy-done.2
  153.6 25.3 %reduce_ladder.1 = f32[4,4,4]{2,1,0:T(4,128)} custom-call(f32[3,64,64]{2,1,0:T(8,128)} %copy-done.2), custom_call_target="tpu_custom_call" | custom-call | tf_op jit(solution)/shard_map/reduce_ladder/pallas_call | solution.py:214
  178.8 1.3 copy.29
  (7 shorter events, 0.1 us)
Async XLA Ops:
  6.5 137.8 %all-gather.2.cloned.1.call-start = ((), (), s32[]{:S(2)}) async-start(), calls=%async_computation | async-start | bytes 2228224 | tf_op jit(solution)/shard_map/all_gather | solution.py:253
  12.1 12.6 %collective-permute-start = (bf16[64,64]{1,0:T(8,128)(2,1)S(1)}, bf16[64,64]{1,0:T(8,128)(2,1)S(1)}, u32[]{:S(2)}, u32[]{:S(2)}) collective-permute-start(bf16[64,64]{1,0:T(8,128)(2,1)S(1)} %fusion.6), channel_id=1, source_target_pairs={{0,0},{1,16},{2,32},{3,48},{4,64},{5,80},{6,96},{7,112},{8,128},{9... | collective-permute-start | bytes 24584 | tf_op jit(solution)/shard_map/ppermute | solution.py:245
  24.7 30.9 %copy-start.3 = (s32[16]{0:T(128)S(1)}, s32[16]{0:T(128)}, u32[]{:S(2)}) copy-start(s32[16]{0:T(128)} %irrep.1) | copy-start | bytes 196
  25.7 30.8 %copy-start.1 = (bf16[192,4096]{1,0:T(8,128)(2,1)S(1)}, bf16[192,4096]{1,0:T(8,128)(2,1)}, u32[]{:S(2)}) copy-start(bf16[192,4096]{1,0:T(8,128)(2,1)} %f_hbm.1) | copy-start | bytes 4718596
  56.5 25.5 %copy-start.4 = (u32[256]{0:T(256)S(1)}, u32[256]{0:T(256)}, u32[]{:S(2)}) copy-start(u32[256]{0:T(256)} %constant.35) | copy-start | bytes 3076
  144.3 1.6 copy-start
  152.9 0.6 copy-start.2
Sparse Core Ops, SparseCore 0:
  55.7 52.6 all-gather.1

commit v2 on v0

v2 whole, which is shorter than its diff:
```python
import jax
import jax.numpy as jnp
from jax import lax
from jax.experimental import pallas as pl
from jax.experimental.pallas import tpu as pltpu
from jax.sharding import PartitionSpec as P

MESH = pl.DeviceIdType.MESH
F32 = jnp.float32
BF16 = jnp.bfloat16
NN = (((1,), (0,)), ((), ()))
NT_DIMS = (((1,), (1,)), ((), ()))
TN = (((0,), (0,)), ((), ()))


def product(left, right, dims=NN):
    return lax.dot_general(left, right, dims, preferred_element_type=F32)


def row_swap():
    at = lax.broadcasted_iota(jnp.int32, (256, 256), 0)
    come = lax.broadcasted_iota(jnp.int32, (256, 256), 1)
    hit = (at // 16 == come % 16) & (at % 16 == come // 16)
    return jnp.where(hit, 1.0, 0.0).astype(BF16)


def regroup(fin, sbuf, g, swap):
    low = lax.broadcasted_iota(jnp.int32, (16, 128), 1) < 64
    for jb in range(2):
        stacks = ([], [])
        for jj in range(16):
            cols = pl.ds(128 * (16 * jb + jj), 128)
            halves = ([], [])
            for kp in range(2):
                v0 = fin[pl.ds(64 * g + 32 * kp, 16), cols].astype(F32)
                v1 = fin[pl.ds(64 * g + 32 * kp + 16, 16), cols].astype(F32)
                halves[0].append(jnp.where(low, v0, pltpu.roll(v1, 64, 1)).astype(BF16))
                halves[1].append(jnp.where(low, pltpu.roll(v0, 64, 1), v1).astype(BF16))
            for e in range(2):
                stacks[e].append(jnp.concatenate(halves[e], axis=1))
        for e in range(2):
            moved = product(swap, jnp.concatenate(stacks[e], axis=0)).astype(BF16)
            for r in range(16):
                sbuf[g, r, pl.ds(32 * e + 16 * jb, 16), :] = moved[16 * r : 16 * r + 16, :]


def own_tiles(mask, irrep, amps, ktile, gtile, dvec, row, col):
    at = lax.broadcasted_iota(jnp.int32, (64, 64), 0)
    to = lax.broadcasted_iota(jnp.int32, (64, 64), 1)
    left = jnp.where(to == 2 * (at % 32) + at // 32, 1.0, 0.0).astype(BF16)
    at = lax.broadcasted_iota(jnp.int32, (64, 128), 0)
    to = lax.broadcasted_iota(jnp.int32, (64, 128), 1)
    within = to % 64
    right = jnp.where(at == 2 * (within % 32) + within // 32, 1.0, 0.0).astype(BF16)
    crossed = jnp.abs(irrep[row].astype(F32) - irrep[col].astype(F32))
    stored = mask[row, col].astype(F32)
    alike = stored * (1.0 - crossed)
    unlike = stored * crossed
    upper = (row <= col).astype(F32)
    lower = 1.0 - upper
    a0, a1, a2, a3 = (amps[p].astype(F32) for p in range(4))
    kept = ((alike * upper) * a0 + (alike * lower) * a3 + unlike * a1).astype(BF16)
    given = ((alike * upper) * a3 + (alike * lower) * a0 + unlike * a2).astype(BF16)
    kept_turned = product(product(left, kept, NT_DIMS).astype(BF16), right)
    kept_plain = product(product(left, kept).astype(BF16), right)
    given_turned = product(product(left, given, NT_DIMS).astype(BF16), right)
    given_plain = product(product(left, given).astype(BF16), right)
    both = jnp.where(
        within < at, kept_turned + kept_plain, jnp.where(within > at, given_turned + given_plain, kept_plain)
    )
    on_diagonal = (row == col).astype(F32)
    mine = on_diagonal * both + (1.0 - on_diagonal) * kept_turned
    half = to // 64
    mine = jnp.where(half == row % 2, mine, 0.0).astype(BF16)
    theirs = jnp.where(half == col % 2, given_plain, 0.0).astype(BF16)
    for h in range(2):
        ktile[h] = mine[32 * h : 32 * h + 32, :]
        gtile[h] = theirs[32 * h : 32 * h + 32, :]
    line = jnp.sum(jnp.where(within == at, given_plain, 0.0), axis=0, keepdims=True)
    dvec[...] = jnp.broadcast_to(line, (8, 128)).astype(BF16)


def split_matrix(irrep, nt, dall, u0, u3, u1):
    lane = lax.broadcasted_iota(jnp.int32, (1, 1024), 1)
    lane2 = lax.broadcasted_iota(jnp.int32, (64, 128), 1)
    row2 = lax.broadcasted_iota(jnp.int32, (64, 128), 0)
    lane_irrep = jnp.zeros((1, 1024), F32)
    for t in range(16):
        lane_irrep = jnp.where(lane // 64 == t, irrep[t].astype(F32), lane_irrep)
    for t in range(16):
        differs = jnp.abs(lane_irrep - irrep[t].astype(F32))
        same = 1.0 - differs
        pair = slice(128 * (t // 2), 128 * (t // 2) + 128)
        same_here = jnp.broadcast_to(same[:, pair], (64, 128))
        offset = lane2 - 64 * (t % 2)
        in_tile = (offset >= 0) & (offset < 64)
        keep0 = (offset < 0) | (in_tile & (offset <= row2))
        keep3 = (offset >= 64) | (in_tile & (offset > row2))
        extra = jnp.where(offset == row2, jnp.broadcast_to(dall[t, 0:1, :].astype(F32), (64, 128)), 0.0).astype(BF16)
        part0 = jnp.where(lane < 64 * t, same, 0.0).astype(BF16)
        part3 = jnp.where(lane >= 64 * (t + 1), same, 0.0).astype(BF16)
        part1 = differs.astype(BF16)
        here0 = jnp.where(keep0, same_here, 0.0).astype(BF16)
        here3 = jnp.where(keep3, same_here, 0.0).astype(BF16)
        for h in range(2):
            rows = pl.ds(64 * t + 32 * h, 32)
            sub = slice(32 * h, 32 * h + 32)
            tile = nt[2 * t + h]
            u1[rows, :] = tile * part1
            u0[rows, :] = tile * part0
            u3[rows, :] = tile * part3
            u0[rows, pair] = tile[:, pair] * here0[sub]
            u3[rows, pair] = tile[:, pair] * here3[sub] + extra[sub]


def chunk_sums(near, u0, u3, u1, xt, acc):
    for i in range(4):
        rows = pl.ds(256 * i, 256)
        done = 256 * (i + 1)
        xt[rows, 0:256] = product(u0[rows, :done], near[:done, :]).astype(BF16)
        xt[rows, 256:512] = product(u3[rows, 256 * i :], near[256 * i :, :]).astype(BF16)
        xt[rows, 512:768] = product(u1[rows, :], near[...]).astype(BF16)
    acc[...] += product(near[...], xt[...], TN)


def kernel(
    mask, irrep, amps_hbm, f_hbm, out,
    amps, fin, sbuf, fm, ktile, gtile, kslot, gslot, dvec, dcol, dall, block, nt, u0, u3, u1, xt, acc,
    send_a, recv_a, send_b, recv_b,
    in_sem, f_send, f_recv, own_sem, k_sem, g_send, g_recv, d_send, d_recv, e_send, e_recv, b_send, b_recv,
    z_send, z_recv, y_send, y_recv, s_send, s_recv, sa, ra, sb, rb,
):
    row = lax.axis_index("row")
    col = lax.axis_index("col")
    half = row % 2
    chip = row // 2
    zhi = col // 4
    yat = col % 4
    sibling = row + 1 - 2 * half

    def remote(src, dst, send, recv, dest):
        return pltpu.make_async_remote_copy(
            src_ref=src, dst_ref=dst, send_sem=send, recv_sem=recv, device_id=dest, device_id_type=MESH
        )

    loads = [pltpu.make_async_copy(amps_hbm, amps, in_sem.at[3])]
    for g in range(3):
        loads.append(pltpu.make_async_copy(f_hbm.at[pl.ds(64 * g, 64)], fin.at[pl.ds(64 * g, 64)], in_sem.at[g]))
    for load in loads:
        load.start()

    barrier = pltpu.get_barrier_semaphore()

    def greet(peer):
        pl.semaphore_signal(barrier, inc=1, device_id=peer, device_id_type=MESH)

    for o in range(1, 16):
        greet(((row + o) % 16, col))
        greet((row, (col + o) % 16))
    for s in range(2):
        @pl.when(2 * chip + s != col)
        def _():
            greet((col, 2 * chip + s))

    loads[0].wait()
    own_tiles(mask, irrep, amps, ktile, gtile, dvec, row, col)
    for s in range(2):
        @pl.when(2 * chip + s == col)
        def _():
            gslot[s] = jnp.zeros((32, 128), BF16)

    pl.semaphore_wait(barrier, jnp.where(row == col, 30, 32))

    k_copy = remote(ktile.at[1 - half], kslot, k_sem.at[0], k_sem.at[1], (sibling, col))
    k_copy.start()
    g_copies = [
        remote(gtile.at[h], gslot.at[col % 2], g_send.at[h], g_recv.at[col % 2], (2 * (col // 2) + h, row))
        for h in range(2)
    ]
    d_copies = [remote(dvec, dcol, d_send.at[o], d_recv, (row, (row + o) % 16)) for o in range(1, 16)]

    @pl.when(row != col)
    def _():
        for copy in g_copies:
            copy.start()

    @pl.when(row == col)
    def _():
        dcol[...] = dvec[...]
        for copy in d_copies:
            copy.start()

    swap = row_swap()
    f_copies = [[], [], []]

    def send_factors(g):
        loads[1 + g].wait()
        regroup(fin, sbuf, g, swap)
        own = pltpu.make_async_copy(sbuf.at[g, row], fm.at[g, pl.ds(pl.multiple_of(64 * row, 64), 64)], own_sem.at[g])
        own.start()
        for o in range(1, 16):
            dest = (row + o) % 16
            copy = remote(
                sbuf.at[g, dest], fm.at[g, pl.ds(pl.multiple_of(64 * row, 64), 64)],
                f_send.at[g, o], f_recv.at[g, o], (dest, col),
            )
            copy.start()
            f_copies[g].append(copy)
        f_copies[g].append(own)

    send_factors(0)

    k_copy.wait_recv()
    for s in range(2):
        @pl.when(2 * chip + s != col)
        def _():
            remote(gtile.at[s], gslot.at[s], g_send.at[s], g_recv.at[s], (sibling, col)).wait_recv()
    summed = ktile[half].astype(F32) + kslot[...].astype(F32) + gslot[0].astype(F32) + gslot[1].astype(F32)
    block[...] = summed.astype(BF16)
    lanes = pl.ds(pl.multiple_of(128 * chip, 128), 128)
    mine = 2 * col + half
    nt[mine, :, lanes] = block[...]
    b_copies = []
    for o in range(1, 8):
        copy = remote(
            block, nt.at[mine, :, lanes], b_send.at[o], b_recv.at[o], (2 * ((chip + o) % 8) + half, col)
        )
        copy.start()
        b_copies.append(copy)

    @pl.when(row != col)
    def _():
        d_copies[0].wait_recv()

    dall[row] = dcol[...]
    e_copies = []
    for o in range(1, 16):
        copy = remote(dcol, dall.at[row], e_send.at[o], e_recv.at[o], ((row + o) % 16, col))
        copy.start()
        e_copies.append(copy)

    send_factors(1)

    for copy in b_copies:
        copy.wait_recv()

    m_copies = []

    def to_y(k, piece):
        for o in range(1, 4):
            copy = remote(
                nt.at[piece], nt.at[piece], y_send.at[k, o], y_recv.at[k, o], (row, 4 * zhi + (yat + o) % 4)
            )
            copy.start()
            m_copies.append(copy)

    def to_sibling(at, piece):
        copy = remote(nt.at[piece], nt.at[piece], s_send.at[at], s_recv.at[at], (sibling, col))
        copy.start()
        m_copies.append(copy)

    z_copies = []
    for o in range(1, 4):
        copy = remote(
            nt.at[mine], nt.at[mine], z_send.at[o], z_recv.at[o], (row, 4 * ((zhi + o) % 4) + yat)
        )
        copy.start()
        z_copies.append(copy)
    to_y(0, mine)
    to_sibling(0, mine)

    send_factors(2)

    for k in range(1, 4):
        z_copies[k - 1].wait_recv()
        piece = 2 * (4 * ((zhi + 4 - k) % 4) + yat) + half
        to_y(k, piece)
        to_sibling(4 * k, piece)
    for k in range(4):
        for o in range(1, 4):
            piece = 2 * (4 * ((zhi + 4 - k) % 4) + (yat + 4 - o) % 4) + half
            remote(
                nt.at[piece], nt.at[piece], y_send.at[k, o], y_recv.at[k, o], (sibling, col)
            ).wait_recv()
            to_sibling(4 * k + o, piece)
    for copy in e_copies:
        copy.wait_recv()
    for at in range(16):
        k, o = at // 4, at % 4
        piece = 2 * (4 * ((zhi + 4 - k) % 4) + (yat + 4 - o) % 4) + 1 - half
        remote(nt.at[piece], nt.at[piece], s_send.at[at], s_recv.at[at], (sibling, col)).wait_recv()

    split_matrix(irrep, nt, dall, u0, u3, u1)
    acc[...] = jnp.zeros_like(acc)
    for g in range(3):
        for copy in f_copies[g][:15]:
            copy.wait_recv()
        f_copies[g][15].wait()
        chunk_sums(fm.at[g], u0, u3, u1, xt, acc)

    sums = []
    for p in range(3):
        total = jnp.zeros((64, 64), F32)
        for k in range(4):
            total = total + acc[64 * k : 64 * k + 64, 256 * p + 64 * k : 256 * p + 64 * k + 64]
        sums.append(total)
    near = (sums[0] + sums[0].T, sums[2].T, sums[2], sums[1] + sums[1].T)
    for r in range(16):
        for p in range(4):
            send_a[r, 4 * p : 4 * p + 4, :] = near[p][4 * r : 4 * r + 4, :]
    a_copies = []
    for o in range(1, 16):
        dest = (row + o) % 16
        copy = remote(send_a.at[dest], recv_a.at[o], sa.at[o], ra.at[o], (dest, col))
        copy.start()
        a_copies.append(copy)
    total = send_a[row]
    for o in range(1, 16):
        a_copies[o - 1].wait_recv()
        total = total + recv_a[o]
    turned = total.T
    for c in range(16):
        send_b[c] = turned[4 * c : 4 * c + 4, :]
    c_copies = []
    for o in range(1, 16):
        dest = (col + o) % 16
        copy = remote(send_b.at[dest], recv_b.at[o], sb.at[o], rb.at[o], (row, dest))
        copy.start()
        c_copies.append(copy)
    final = send_b[col]
    for o in range(1, 16):
        c_copies[o - 1].wait_recv()
        final = final + recv_b[o]
    back = final.T
    for p in range(4):
        out[p] = back[4 * p : 4 * p + 4, :]

    k_copy.wait_send()

    @pl.when(row != col)
    def _():
        for copy in g_copies:
            copy.wait_send()

    @pl.when(row == col)
    def _():
        for copy in d_copies:
            copy.wait_send()

    for copies in (f_copies[0][:15], f_copies[1][:15], f_copies[2][:15], b_copies, e_copies, z_copies, m_copies,
                   a_copies, c_copies):
        for copy in copies:
            copy.wait_send()


def per_device(amplitudes, factors, tile_mask, tile_irrep):
    smem = pl.BlockSpec(memory_space=pltpu.SMEM)
    place = pl.BlockSpec(memory_space=pl.ANY)
    dma = pltpu.SemaphoreType.DMA
    return pl.pallas_call(
        kernel,
        out_shape=jax.ShapeDtypeStruct((4, 4, 4), F32),
        in_specs=[smem, smem, place, place],
        out_specs=pl.BlockSpec(memory_space=pltpu.VMEM),
        scratch_shapes=[
            pltpu.VMEM((4, 64, 64), BF16),
            pltpu.VMEM((192, 4096), BF16),
            pltpu.VMEM((3, 16, 64, 256), BF16),
            pltpu.VMEM((3, 1024, 256), BF16),
            pltpu.VMEM((2, 32, 128), BF16),
            pltpu.VMEM((2, 32, 128), BF16),
            pltpu.VMEM((32, 128), BF16),
            pltpu.VMEM((2, 32, 128), BF16),
            pltpu.VMEM((8, 128), BF16),
            pltpu.VMEM((8, 128), BF16),
            pltpu.VMEM((16, 8, 128), BF16),
            pltpu.VMEM((32, 128), BF16),
            pltpu.VMEM((32, 32, 1024), BF16),
            pltpu.VMEM((1024, 1024), BF16),
            pltpu.VMEM((1024, 1024), BF16),
            pltpu.VMEM((1024, 1024), BF16),
            pltpu.VMEM((1024, 768), BF16),
            pltpu.VMEM((256, 768), F32),
            pltpu.VMEM((16, 16, 64), F32),
            pltpu.VMEM((16, 16, 64), F32),
            pltpu.VMEM((16, 4, 16), F32),
            pltpu.VMEM((16, 4, 16), F32),
            dma((4,)), dma((3, 16)), dma((3, 16)), dma((3,)), dma((2,)), dma((2,)), dma((2,)),
            dma((16,)), dma(()), dma((16,)), dma((16,)), dma((8,)), dma((8,)),
            dma((4,)), dma((4,)), dma((4, 4)), dma((4, 4)), dma((16,)), dma((16,)),
            dma((16,)), dma((16,)), dma((16,)), dma((16,)),
        ],
        compiler_params=pltpu.CompilerParams(collective_id=0, has_side_effects=True, vmem_limit_bytes=48 << 20),
        name="ladder",
    )(tile_mask, tile_irrep, amplitudes, factors)


def solution(mesh):
    return jax.shard_map(
        per_device,
        mesh=mesh,
        in_specs=(P(None, "row", "col"), P("col", "row"), P(), P()),
        out_specs=P(None, "row", "col"),
        check_vma=False,
    )
```

time: 612 us -> 66.6 us (0.11)
  waiting for transfers between devices: 243 us -> 0 us
  blocking collectives: 155 us -> 0 us
  local copies, waits for them, and re-layouts: 99.9 us -> 4.2 us
  matrix products: 74.7 us -> 0 us
  Pallas kernels: 0 us -> 62.1 us
  between operations: 14.8 us -> 0.01 us
  starting transfers between devices: 14.7 us -> 0 us
    unnamed x3 -> x0, waiting for transfers between devices: 153 us -> none
    all_gather x2 -> x0, blocking collectives: 95.2 us -> none  [the longest x1 55.8 us: per_device(): amp_row = lax.all_gather(amplitudes, 'col', axis=2, tiled=True)]
    all_gather x1 -> x0, waiting for transfers between devices: 83.9 us -> none  [per_device(): far_all = lax.all_gather(factors, 'row', axis=1, tiled=True)]
    dot_general x12 -> x0, matrix products: 74.7 us -> none  [one_block(): jnp.einsum('qpkad,qdb->pab', partial_value, far_block, preferred_element_...]
    pallas_call x0 -> x1, Pallas kernels: none -> 62.1 us  [per_device(): pl.pallas_call(kernel, out_shape=jax.ShapeDtypeStruct((4, 4, 4), F32), in...]
    unnamed x1 -> x0, blocking collectives: 60.3 us -> none
    unnamed x15 -> x9, local copies, waits for them, and re-layouts: 61.8 us -> 4.2 us
    all_gather x1 -> x0, local copies, waits for them, and re-layouts: 36.1 us -> none  [per_device(): far_all = lax.all_gather(factors, 'row', axis=1, tiled=True)]
  transfers between devices with their start and end apart: 3 -> 0, of which waited for: 3 -> 0; matrix products, arithmetic and copies ran while one was open for 3% -> 0% of each run, Pallas kernels for 0% -> 0%
where the time goes in v2:
time: 66.6 us; the launch traced here: 66.4 us
  Pallas kernels  62.1 us (93%)
  local copies, waits for them, and re-layouts  4.2 us (6%)
    pallas_call x1, Pallas kernels, per_device(): pl.pallas_call(kernel, out_shape=jax.ShapeDtypeStruct((4, 4, 4), F32), in...  62.1 us
    unnamed x9, local copies, waits for them, and re-layouts  4.2 us

profile of v2, /device:TPU:1, one launch (start us, length us, event | category | flops | bytes accessed | tf_op | source)
XLA Modules:
  0.0 66.4 jit_solution(8673598331878694330)
XLA Ops:
  0.0 0.0 copy-start
  0.0 1.4 %copy-done = bf16[192,4096]{1,0:T(8,128)(2,1)S(1)} copy-done((bf16[192,4096]{1,0:T(8,128)(2,1)S(1)}, bf16[192,4096]{1,0:T(8,128)(2,1)}, u32[]{:S(2)}) %copy-start) | copy-done | bytes 1572888
  1.4 0.0 copy-start.1
  1.4 0.8 %copy-done.1 = bf16[4,64,64]{2,1,0:T(8,128)(2,1)S(1)} copy-done((bf16[4,64,64]{2,1,0:T(8,128)(2,1)S(1)}, bf16[4,64,64]{2,1,0:T(8,128)(2,1)}, u32[]{:S(2)}) %copy-start.1) | copy-done | bytes 32792
  2.2 0.0 copy-start.2
  2.3 0.7 %copy-done.2 = s32[16,16]{1,0:T(8,128)S(1)} copy-done((s32[16,16]{1,0:T(8,128)S(1)}, s32[16,16]{1,0:T(8,128)}, u32[]{:S(2)}) %copy-start.2) | copy-done | bytes 1048
  2.9 0.0 copy-start.3
  2.9 0.7 copy-done.3
  3.6 62.1 %ladder.1 = f32[4,4,4]{2,1,0:T(4,128)S(1)} custom-call(s32[16,16]{1,0:T(8,128)S(1)} %copy-done.2, s32[16]{0:T(128)S(1)} %copy-done.3, bf16[4,64,64]{2,1,0:T(8,128)(2,1)S(1)} %copy-done.1, bf16[192,4096]{1,0:T(8,128)(2,1)S(1)} %copy-done), custom_call_target="tpu_custom_call" | custom-call | tf_op jit(solution)/shard_map/ladder/pallas_call | solution.py:360
  65.8 0.6 copy.6
Async XLA Ops:
  0.0 1.4 %copy-start = (bf16[192,4096]{1,0:T(8,128)(2,1)S(1)}, bf16[192,4096]{1,0:T(8,128)(2,1)}, u32[]{:S(2)}) copy-start(bf16[192,4096]{1,0:T(8,128)(2,1)} %f_hbm.1) | copy-start | bytes 4718596
  1.4 0.8 %copy-start.1 = (bf16[4,64,64]{2,1,0:T(8,128)(2,1)S(1)}, bf16[4,64,64]{2,1,0:T(8,128)(2,1)}, u32[]{:S(2)}) copy-start(bf16[4,64,64]{2,1,0:T(8,128)(2,1)} %amps_hbm.1) | copy-start | bytes 98308
  2.2 0.7 %copy-start.2 = (s32[16,16]{1,0:T(8,128)S(1)}, s32[16,16]{1,0:T(8,128)}, u32[]{:S(2)}) copy-start(s32[16,16]{1,0:T(8,128)} %mask.1) | copy-start | bytes 3076
  2.9 0.7 copy-start.3

commit v3 on v2

v3 whole, which is shorter than its diff:
```python
import jax
import jax.numpy as jnp
from jax import lax
from jax.experimental import pallas as pl
from jax.experimental.pallas import tpu as pltpu
from jax.sharding import PartitionSpec as P

MESH = pl.DeviceIdType.MESH
F32 = jnp.float32
BF16 = jnp.bfloat16
NN = (((1,), (0,)), ((), ()))
NT_DIMS = (((1,), (1,)), ((), ()))
TN = (((0,), (0,)), ((), ()))


def product(left, right, dims=NN):
    return lax.dot_general(left, right, dims, preferred_element_type=F32)


def row_swap():
    at = lax.broadcasted_iota(jnp.int32, (256, 256), 0)
    come = lax.broadcasted_iota(jnp.int32, (256, 256), 1)
    hit = (at // 16 == come % 16) & (at % 16 == come // 16)
    return jnp.where(hit, 1.0, 0.0).astype(BF16)


def regroup(fin, sbuf, g, swap):
    low = lax.broadcasted_iota(jnp.int32, (16, 128), 1) < 64
    for jb in range(2):
        stacks = ([], [])
        for jj in range(16):
            cols = pl.ds(128 * (16 * jb + jj), 128)
            halves = ([], [])
            for kp in range(2):
                v0 = fin[pl.ds(64 * g + 32 * kp, 16), cols].astype(F32)
                v1 = fin[pl.ds(64 * g + 32 * kp + 16, 16), cols].astype(F32)
                halves[0].append(jnp.where(low, v0, pltpu.roll(v1, 64, 1)).astype(BF16))
                halves[1].append(jnp.where(low, pltpu.roll(v0, 64, 1), v1).astype(BF16))
            for e in range(2):
                stacks[e].append(jnp.concatenate(halves[e], axis=1))
        for e in range(2):
            moved = product(swap, jnp.concatenate(stacks[e], axis=0)).astype(BF16)
            for r in range(16):
                sbuf[r, g, pl.ds(32 * e + 16 * jb, 16), :] = moved[16 * r : 16 * r + 16, :]


def unpacked(ref, side):
    low = lax.broadcasted_iota(jnp.int32, (16, 128), 1) < 64
    packed = ref[...].astype(F32)
    turned = pltpu.roll(packed, 64, 1)
    rows = jnp.concatenate([jnp.where(low, packed, turned), jnp.where(low, turned, packed)], axis=0)
    lane = lax.broadcasted_iota(jnp.int32, (32, 128), 1)
    return jnp.where(lane // 64 == side, rows, 0.0)


def own_tiles(mask, irrep, amps, kfull, ktile, gtile, dvec, row, col):
    at = lax.broadcasted_iota(jnp.int32, (64, 64), 0)
    to = lax.broadcasted_iota(jnp.int32, (64, 64), 1)
    left = jnp.where(to == 2 * (at % 32) + at // 32, 1.0, 0.0).astype(BF16)
    at = lax.broadcasted_iota(jnp.int32, (64, 128), 0)
    to = lax.broadcasted_iota(jnp.int32, (64, 128), 1)
    within = to % 64
    right = jnp.where(at == 2 * (within % 32) + within // 32, 1.0, 0.0).astype(BF16)
    crossed = jnp.abs(irrep[row].astype(F32) - irrep[col].astype(F32))
    stored = mask[row, col].astype(F32)
    alike = stored * (1.0 - crossed)
    unlike = stored * crossed
    upper = (row <= col).astype(F32)
    lower = 1.0 - upper
    a0, a1, a2, a3 = (amps[p].astype(F32) for p in range(4))
    kept = ((alike * upper) * a0 + (alike * lower) * a3 + unlike * a1).astype(BF16)
    given = ((alike * upper) * a3 + (alike * lower) * a0 + unlike * a2).astype(BF16)
    kept_turned = product(product(left, kept, NT_DIMS).astype(BF16), right)
    kept_plain = product(product(left, kept).astype(BF16), right)
    given_turned = product(product(left, given, NT_DIMS).astype(BF16), right)
    given_plain = product(product(left, given).astype(BF16), right)
    both = jnp.where(
        within < at, kept_turned + kept_plain, jnp.where(within > at, given_turned + given_plain, kept_plain)
    )
    on_diagonal = (row == col).astype(F32)
    mine = on_diagonal * both + (1.0 - on_diagonal) * kept_turned
    low = lax.broadcasted_iota(jnp.int32, (16, 128), 1) < 64
    for h in range(2):
        at_h = 32 * h
        kfull[h] = jnp.where(to[:32] // 64 == row % 2, mine[at_h : at_h + 32], 0.0)
        ktile[h] = jnp.where(low, mine[at_h : at_h + 16], mine[at_h + 16 : at_h + 32]).astype(BF16)
        gtile[h] = jnp.where(low, given_plain[at_h : at_h + 16], given_plain[at_h + 16 : at_h + 32]).astype(BF16)
    line = jnp.sum(jnp.where(to == at, given_plain, 0.0), axis=1, keepdims=True)
    dvec[...] = jnp.broadcast_to(line, (64, 128)).astype(BF16)


def lane_irreps(irrep):
    lane = lax.broadcasted_iota(jnp.int32, (1, 1024), 1)
    out = jnp.zeros((1, 1024), F32)
    for t in range(16):
        out = jnp.where(lane // 64 == t, irrep[t].astype(F32), out)
    return out


def split_rows(i, chip, irrep, of_lane, nt, u0, u3, u1):
    bits = (chip // 4, chip // 2 % 2, chip % 2)
    place = []
    for j in range(8):
        offsets = [1 - bit if (j >> (2 - n)) & 1 else bit for n, bit in enumerate(bits)]
        place.append(4 * offsets[0] + 2 * offsets[1] + offsets[2])
    lane2 = lax.broadcasted_iota(jnp.int32, (64, 128), 1)
    row2 = lax.broadcasted_iota(jnp.int32, (64, 128), 0)
    for y in range(4):
        t = 4 * i + y
        differs = jnp.abs(of_lane - irrep[t].astype(F32))
        same = 1.0 - differs
        offset = lane2 - 64 * (t % 2)
        in_tile = (offset >= 0) & (offset < 64)
        here = jnp.broadcast_to(same[:, 128 * (t // 2) : 128 * (t // 2) + 128], (64, 128))
        here0 = jnp.where((offset < 0) | (in_tile & (offset <= row2)), here, 0.0).astype(BF16)
        here3 = jnp.where((offset >= 64) | (in_tile & (offset > row2)), here, 0.0).astype(BF16)
        alike = same.astype(BF16)
        unlike = differs.astype(BF16)
        for h in range(2):
            rows = pl.ds(64 * t + 32 * h, 32)
            sub = slice(32 * h, 32 * h + 32)
            for j in range(8):
                lanes = slice(128 * j, 128 * j + 128)
                tile = nt[h, y, place[j], i]
                u1[rows, lanes] = tile * unlike[:, lanes]
                if j == t // 2:
                    u0[rows, lanes] = tile * here0[sub]
                    u3[rows, lanes] = tile * here3[sub]
                elif j < t // 2:
                    u0[rows, lanes] = tile * alike[:, lanes]
                    if j >= 2 * i:
                        u3[rows, lanes] = jnp.zeros((32, 128), BF16)
                else:
                    u3[rows, lanes] = tile * alike[:, lanes]
                    if j < 2 * i + 2:
                        u0[rows, lanes] = jnp.zeros((32, 128), BF16)


def row_sums(i, near, u0, u3, u1, acc):
    rows = pl.ds(256 * i, 256)
    done = 256 * (i + 1)
    x0 = product(u0[rows, :done], near[:done, :]).astype(BF16)
    x3 = product(u3[rows, 256 * i :], near[256 * i :, :]).astype(BF16)
    x1 = product(u1[rows, :], near[...]).astype(BF16)
    acc[...] += product(near[rows, :], jnp.concatenate([x0, x3, x1], axis=1), TN)


def kernel(
    mask_hbm, irrep_hbm, amps_hbm, f_hbm, out,
    mask, irrep, amps, fin, sbuf, fm, kfull, ktile, gtile, kslot, gslot, dvec, dcol, nt, u0, u3, u1, acc,
    send_a, recv_a, send_b, recv_b,
    in_sem, f_send, f_recv, own_sem, k_sem, g_send, g_recv, d_send, d_recv, b_send, b_recv,
    z_send, z_recv, y_send, y_recv, s_send, s_recv, sa, ra, sb, rb,
):
    row = lax.axis_index("row")
    col = lax.axis_index("col")
    half = row % 2
    chip = row // 2
    zhi = col // 4
    yat = col % 4
    sibling = row + 1 - 2 * half

    def remote(src, dst, send, recv, dest):
        return pltpu.make_async_remote_copy(
            src_ref=src, dst_ref=dst, send_sem=send, recv_sem=recv, device_id=dest, device_id_type=MESH
        )

    loads = [
        pltpu.make_async_copy(amps_hbm, amps, in_sem.at[3]),
        pltpu.make_async_copy(mask_hbm, mask, in_sem.at[4]),
        pltpu.make_async_copy(irrep_hbm, irrep, in_sem.at[5]),
    ]
    for g in range(3):
        loads.append(pltpu.make_async_copy(f_hbm.at[pl.ds(64 * g, 64)], fin.at[pl.ds(64 * g, 64)], in_sem.at[g]))
    for load in loads:
        load.start()

    barrier = pltpu.get_barrier_semaphore()

    def greet(peer):
        pl.semaphore_signal(barrier, inc=1, device_id=peer, device_id_type=MESH)

    for o in range(1, 16):
        greet(((row + o) % 16, col))
        greet((row, (col + o) % 16))
    for s in range(2):
        @pl.when(2 * chip + s != col)
        def _():
            greet((col, 2 * chip + s))

    for load in loads[:3]:
        load.wait()
    own_tiles(mask, irrep, amps, kfull, ktile, gtile, dvec, row, col)
    for s in range(2):
        @pl.when(2 * chip + s == col)
        def _():
            gslot[s] = jnp.zeros((16, 128), BF16)
    pl.semaphore_wait(barrier, jnp.where(row == col, 30, 32))

    k_copy = remote(ktile.at[1 - half], kslot, k_sem.at[0], k_sem.at[1], (sibling, col))
    k_copy.start()
    g_copies = [
        remote(gtile.at[h], gslot.at[col % 2], g_send.at[h], g_recv.at[col % 2], (2 * (col // 2) + h, row))
        for h in range(2)
    ]
    d_copies = [remote(dvec, dcol, d_send.at[o], d_recv, (row, (row + o) % 16)) for o in range(1, 16)]

    @pl.when(row != col)
    def _():
        for copy in g_copies:
            copy.start()

    swap = row_swap()
    f_copies = [[], [], []]

    def send_factors(part):
        first, count = part, 1
        for g in range(first, first + count):
            loads[3 + g].wait()
            regroup(fin, sbuf, g, swap)
        groups = pl.ds(first, count)
        place = pl.ds(pl.multiple_of(64 * row, 64), 64)
        for o in range(1, 16):
            dest = (row + o) % 16
            copy = remote(
                sbuf.at[dest, groups], fm.at[groups, place], f_send.at[part, o], f_recv.at[part, o], (dest, col)
            )
            copy.start()
            f_copies[part].append(copy)
        copy = pltpu.make_async_copy(sbuf.at[row, groups], fm.at[groups, place], own_sem.at[part])
        copy.start()
        f_copies[part].append(copy)

    send_factors(0)
    of_lane = lane_irreps(irrep)
    acc[...] = jnp.zeros_like(acc)

    k_copy.wait_recv()
    for s in range(2):
        @pl.when(2 * chip + s != col)
        def _():
            remote(gtile.at[s], gslot.at[s], g_send.at[s], g_recv.at[s], (sibling, col)).wait_recv()
    summed = kfull[half] + unpacked(kslot, 1 - half) + unpacked(gslot.at[0], 0) + unpacked(gslot.at[1], 1)
    nt[half, yat, 0, zhi] = summed.astype(BF16)
    z_copies = []
    for o in range(1, 4):
        at = nt.at[half, yat, 0, zhi]
        copy = remote(at, at, z_send.at[o], z_recv.at[o], (row, 4 * ((zhi + o) % 4) + yat))
        copy.start()
        z_copies.append(copy)

    @pl.when(row == col)
    def _():
        dcol[...] = dvec[...]
        for copy in d_copies:
            copy.start()


    for o in range(1, 4):
        at = nt.at[half, yat, 0, (zhi + 4 - o) % 4]
        remote(at, at, z_send.at[o], z_recv.at[o], (sibling, col)).wait_recv()
    xhigh, xlow, zlo = chip // 4, chip // 2 % 2, chip % 2

    def flipped(bit, by):
        return 1 - bit if by else bit

    def at_offset(m):
        return 4 * flipped(xhigh, m // 4) + 2 * flipped(xlow, m // 2 % 2) + flipped(zlo, m % 2)

    b_copies = []
    for m in range(1, 8):
        copy = remote(
            nt.at[half, yat, 0], nt.at[half, yat, m], b_send.at[m], b_recv.at[m], (2 * at_offset(m) + half, col)
        )
        copy.start()
        b_copies.append(copy)

    def piece(h, y, p):
        return nt.at[h, y, p] if p < 2 else nt.at[h, y, pl.ds(2, 6), p - 2]

    y_copies = []
    m_copies = []

    def send_piece(p):
        at = piece(half, yat, p)
        copies = [
            remote(at, at, y_send.at[p, o], y_recv.at[p, o], (row, 4 * zhi + (yat + o) % 4)) for o in range(1, 4)
        ]
        copies.append(remote(at, at, s_send.at[p, 0], s_recv.at[p, 0], (sibling, col)))
        for copy in copies:
            copy.start()
        y_copies.append(copies)

    def take_pieces(pieces):
        for p in pieces:
            for o in range(1, 4):
                at = piece(half, (yat + 4 - o) % 4, p)
                remote(at, at, y_send.at[p, o], y_recv.at[p, o], (sibling, col)).wait_recv()
                copy = remote(at, at, s_send.at[p, o], s_recv.at[p, o], (sibling, col))
                copy.start()
                m_copies.append(copy)
        for p in pieces:
            for o in range(4):
                at = piece(1 - half, (yat + 4 - o) % 4, p)
                remote(at, at, s_send.at[p, o], s_recv.at[p, o], (sibling, col)).wait_recv()

    def factors_here(part):
        f_copies[part][15].wait()
        for copy in f_copies[part][:15]:
            copy.wait_recv()

    send_piece(0)
    b_copies[0].wait_recv()
    send_piece(1)
    send_factors(1)
    for copy in b_copies[1:]:
        copy.wait_recv()
    send_piece(2)
    send_piece(3)
    send_factors(2)

    @pl.when(row != col)
    def _():
        d_copies[0].wait_recv()

    scale = jnp.concatenate([dcol[...], dcol[...]], axis=1)
    diagonal = jnp.zeros((256, 256), F32)
    for g in range(3):
        plain = jnp.concatenate([sbuf[r, g] for r in range(16)], axis=0)
        scaled = jnp.concatenate([sbuf[r, g] * scale for r in range(16)], axis=0)
        diagonal = diagonal + product(scaled, plain, TN)
    acc[:, 256:512] = diagonal

    plan = (
        ((0, 0),),
        ((1, 0), (0, 1), (1, 1)),
        ((2, 0), (2, 1)),
        ((3, 0), (3, 1), (0, 2), (1, 2), (2, 2), (3, 2)),
    )
    arrived = set()
    for i in range(4):
        if i < 2:
            for copy in y_copies[2 + i]:
                copy.wait_send()
            send_piece(4 + i)
        take_pieces((0, 1, 2) if i == 0 else (2 + i,))
        split_rows(i, chip, irrep, of_lane, nt, u0, u3, u1)
        for k, g in plan[i]:
            if g not in arrived:
                arrived.add(g)
                factors_here(g)
            row_sums(k, fm.at[g], u0, u3, u1, acc)
    for p in (0, 1, 4, 5):
        m_copies += y_copies[p]

    sums = []
    for p in range(3):
        total = jnp.zeros((64, 64), F32)
        for k in range(4):
            total = total + acc[64 * k : 64 * k + 64, 256 * p + 64 * k : 256 * p + 64 * k + 64]
        sums.append(total)
    near = (sums[0] + sums[0].T, sums[2].T, sums[2], sums[1] + sums[1].T)
    for r in range(16):
        for p in range(4):
            send_a[r, 4 * p : 4 * p + 4, :] = near[p][4 * r : 4 * r + 4, :]
    a_copies = []
    for o in range(1, 16):
        dest = (row + o) % 16
        copy = remote(send_a.at[dest], recv_a.at[o], sa.at[o], ra.at[o], (dest, col))
        copy.start()
        a_copies.append(copy)
    total = send_a[row]
    for o in range(1, 16):
        a_copies[o - 1].wait_recv()
        total = total + recv_a[o]
    turned = total.T
    for c in range(16):
        send_b[c] = turned[4 * c : 4 * c + 4, :]
    c_copies = []
    for o in range(1, 16):
        dest = (col + o) % 16
        copy = remote(send_b.at[dest], recv_b.at[o], sb.at[o], rb.at[o], (row, dest))
        copy.start()
        c_copies.append(copy)
    final = send_b[col]
    for o in range(1, 16):
        c_copies[o - 1].wait_recv()
        final = final + recv_b[o]
    back = final.T
    for p in range(4):
        out[p] = back[4 * p : 4 * p + 4, :]

    k_copy.wait_send()

    @pl.when(row != col)
    def _():
        for copy in g_copies:
            copy.wait_send()

    @pl.when(row == col)
    def _():
        for copy in d_copies:
            copy.wait_send()

    for copies in (f_copies[0][:15], f_copies[1][:15], f_copies[2][:15], b_copies, z_copies, m_copies,
                   a_copies, c_copies):
        for copy in copies:
            copy.wait_send()


def per_device(amplitudes, factors, tile_mask, tile_irrep):
    place = pl.BlockSpec(memory_space=pltpu.HBM)
    dma = pltpu.SemaphoreType.DMA
    return pl.pallas_call(
        kernel,
        out_shape=jax.ShapeDtypeStruct((4, 4, 4), F32),
        in_specs=[place] * 4,
        out_specs=pl.BlockSpec(memory_space=pltpu.VMEM),
        scratch_shapes=[
            pltpu.SMEM((16, 16), jnp.int32),
            pltpu.SMEM((16,), jnp.int32),
            pltpu.VMEM((4, 64, 64), BF16),
            pltpu.VMEM((192, 4096), BF16),
            pltpu.VMEM((16, 3, 64, 256), BF16),
            pltpu.VMEM((3, 1024, 256), BF16),
            pltpu.VMEM((2, 32, 128), F32),
            pltpu.VMEM((2, 16, 128), BF16),
            pltpu.VMEM((2, 16, 128), BF16),
            pltpu.VMEM((16, 128), BF16),
            pltpu.VMEM((2, 16, 128), BF16),
            pltpu.VMEM((64, 128), BF16),
            pltpu.VMEM((64, 128), BF16),
            pltpu.VMEM((2, 4, 8, 4, 32, 128), BF16),
            pltpu.VMEM((1024, 1024), BF16),
            pltpu.VMEM((1024, 1024), BF16),
            pltpu.VMEM((1024, 1024), BF16),
            pltpu.VMEM((256, 768), F32),
            pltpu.VMEM((16, 16, 64), F32),
            pltpu.VMEM((16, 16, 64), F32),
            pltpu.VMEM((16, 4, 16), F32),
            pltpu.VMEM((16, 4, 16), F32),
            dma((6,)), dma((3, 16)), dma((3, 16)), dma((3,)), dma((2,)), dma((2,)), dma((2,)),
            dma((16,)), dma(()), dma((8,)), dma((8,)),
            dma((4,)), dma((4,)), dma((6, 4)), dma((6, 4)), dma((6, 4)), dma((6, 4)),
            dma((16,)), dma((16,)), dma((16,)), dma((16,)),
        ],
        compiler_params=pltpu.CompilerParams(collective_id=0, has_side_effects=True, vmem_limit_bytes=62 << 20),
        name="ladder",
    )(tile_mask, tile_irrep, amplitudes, factors)


def solution(mesh):
    return jax.shard_map(
        per_device,
        mesh=mesh,
        in_specs=(P(None, "row", "col"), P("col", "row"), P(), P()),
        out_specs=P(None, "row", "col"),
        check_vma=False,
    )
```

time: 66.6 us -> 59.8 us (0.90)
  Pallas kernels: 62.1 us -> 58.3 us
  local copies, waits for them, and re-layouts: 4.2 us -> 1.3 us
    pallas_call x1, Pallas kernels: 62.1 us -> 58.3 us  [per_device(): pl.pallas_call(kernel, out_shape=jax.ShapeDtypeStruct((4, 4, 4), F32), in...]
    unnamed x9 -> x1, local copies, waits for them, and re-layouts: 4.2 us -> 1.3 us
where the time goes in v3:
time: 59.8 us; the launch traced here: 59.6 us
  Pallas kernels  58.3 us (97%)
  local copies, waits for them, and re-layouts  1.3 us (2%)
    pallas_call x1, Pallas kernels, per_device(): pl.pallas_call(kernel, out_shape=jax.ShapeDtypeStruct((4, 4, 4), F32), in...  58.3 us
    unnamed x1, local copies, waits for them, and re-layouts  1.3 us

profile of v3, /device:TPU:1, one launch (start us, length us, event | category | flops | bytes accessed | tf_op | source)
XLA Modules:
  0.0 59.6 jit_solution(11036476974353031010)
XLA Ops:
  0.0 58.3 %ladder.1 = f32[4,4,4]{2,1,0:T(4,128)} custom-call(s32[16,16]{1,0:T(8,128)} %mask_hbm.1, s32[16]{0:T(128)} %irrep_hbm.1, bf16[4,64,64]{2,1,0:T(8,128)(2,1)} %amps_hbm.1, bf16[192,4096]{1,0:T(8,128)(2,1)} %f_hbm.1), custom_call_target="tpu_custom_call" | custom-call | tf_op jit(solution)/shard_map/ladder/pallas_call | solution.py:414
  58.3 1.3 %copy.6 = f32[4,4,4]{2,1,0:T(4,128)} copy(f32[4,4,4]{2,1,0:T(4,128)} %ladder.1) | data formatting | bytes 512

commit v4 on v3

--- a/solution.py
+++ b/solution.py
@@ -215,9 +215,6 @@
 
     def send_factors(part):
         first, count = part, 1
-        for g in range(first, first + count):
-            loads[3 + g].wait()
-            regroup(fin, sbuf, g, swap)
         groups = pl.ds(first, count)
         place = pl.ds(pl.multiple_of(64 * row, 64), 64)
         for o in range(1, 16):
@@ -231,7 +228,11 @@
         copy.start()
         f_copies[part].append(copy)
 
-    send_factors(0)
+    for part in range(3):
+        loads[3 + part].wait()
+        regroup(fin, sbuf, part, swap)
+        if part == 0:
+            send_factors(0)
     of_lane = lane_irreps(irrep)
     acc[...] = jnp.zeros_like(acc)
 
@@ -243,7 +244,7 @@
     summed = kfull[half] + unpacked(kslot, 1 - half) + unpacked(gslot.at[0], 0) + unpacked(gslot.at[1], 1)
     nt[half, yat, 0, zhi] = summed.astype(BF16)
     z_copies = []
-    for o in range(1, 4):
+    for o in (2, 1, 3):
         at = nt.at[half, yat, 0, zhi]
         copy = remote(at, at, z_send.at[o], z_recv.at[o], (row, 4 * ((zhi + o) % 4) + yat))
         copy.start()
@@ -284,7 +285,7 @@
     def send_piece(p):
         at = piece(half, yat, p)
         copies = [
-            remote(at, at, y_send.at[p, o], y_recv.at[p, o], (row, 4 * zhi + (yat + o) % 4)) for o in range(1, 4)
+            remote(at, at, y_send.at[p, o], y_recv.at[p, o], (row, 4 * zhi + (yat + o) % 4)) for o in (2, 1, 3)
         ]
         copies.append(remote(at, at, s_send.at[p, 0], s_recv.at[p, 0], (sibling, col)))
         for copy in copies:

time: 59.8 us -> 59.7 us (level)
  no operation moved by 1% of the time
where the time goes in v4:
time: 59.7 us; the launch traced here: 59.6 us
  Pallas kernels  58.3 us (98%)
  local copies, waits for them, and re-layouts  1.3 us (2%)
    pallas_call x1, Pallas kernels, per_device(): pl.pallas_call(kernel, out_shape=jax.ShapeDtypeStruct((4, 4, 4), F32), in...  58.3 us
    unnamed x1, local copies, waits for them, and re-layouts  1.3 us

profile of v4, /device:TPU:1, one launch (start us, length us, event | category | flops | bytes accessed | tf_op | source)
XLA Modules:
  0.0 59.6 jit_solution(450745968813478381)
XLA Ops:
  0.0 58.3 %ladder.1 = f32[4,4,4]{2,1,0:T(4,128)} custom-call(s32[16,16]{1,0:T(8,128)} %mask_hbm.1, s32[16]{0:T(128)} %irrep_hbm.1, bf16[4,64,64]{2,1,0:T(8,128)(2,1)} %amps_hbm.1, bf16[192,4096]{1,0:T(8,128)(2,1)} %f_hbm.1), custom_call_target="tpu_custom_call" | custom-call | tf_op jit(solution)/shard_map/ladder/pallas_call | solution.py:415
  58.3 1.3 %copy.6 = f32[4,4,4]{2,1,0:T(4,128)} copy(f32[4,4,4]{2,1,0:T(4,128)} %ladder.1) | data formatting | bytes 512
